TPU v7x, 512 devices: a whole 4x4x16 slice. The times are simulated.
512 devices in a mesh: term: 8 (over y, core), doc: 16 (over z), enc: 4 (over x).
Axes of the slice: x: 4, y: 4, z: 16, core: 2. Of those that a mesh axis runs over, the one named last changes fastest.
Arguments:
- query_weights: bfloat16 [1024, 30720], P('enc', ('term', 'doc')), may hold values from 0.049804688 to 2
- tile_terms: int32 [30720], P(('term', 'doc')), may hold values from 0 to 59
- tile_blocks: int32 [30720], P(('term', 'doc')), may hold values from 0 to 15
- tile_counts: int32 [128], P(('term', 'doc')), may hold values from 60 to 240, as said below
- impacts: bfloat16 [30720, 64, 128], P(('term', 'doc')), may hold values from -0.015625 to 0.015625
Outputs:
- scores: float32 [2048, 1024], P('doc', 'enc')
Inputs may be any that keep to these rules, and one draw needn't show every extreme that they name: Slots at positions tile_counts or later of a device's list are padding and contribute nothing; some device has all 240 slots live.
All inputs are finite; a program needn't handle non-finite values.
Results may differ from a plain program's by a relative error of at most 0.0003.
Values may be sent and summed in bfloat16 or wider, within the bound.
No kernel may reach another device: no remote copies, remote signals or barrier semaphores. Data moves between devices by JAX's collectives and lax.ppermute only.
A program may use at most 64 MiB of HBM per device.

v0:
```python
import jax
import jax.numpy as jnp
from jax import lax
from jax.sharding import PartitionSpec as P


def block_size(tiles):
    largest = 1
    for divisor in range(1, 65):
        if tiles % divisor == 0:
            largest = divisor
    return largest


def per_device(query_weights, tile_terms, tile_blocks, tile_counts, impacts):
    range_rows = lax.all_gather(query_weights, "doc", axis=1, tiled=True)
    queries = range_rows.shape[0]
    tiles, term_block, doc_block = impacts.shape
    owners = lax.axis_size("doc")
    grouped = range_rows.reshape(queries, range_rows.shape[1] // term_block, term_block)
    step = block_size(tiles)
    live = jnp.arange(tiles, dtype=jnp.int32) < tile_counts[0]
    owner_ids = jnp.arange(owners, dtype=jnp.int32)

    def accumulate(total, number):
        start = number * step
        term_now = lax.dynamic_slice_in_dim(tile_terms, start, step)
        owner_now = lax.dynamic_slice_in_dim(tile_blocks, start, step)
        keep_now = lax.dynamic_slice_in_dim(live, start, step)
        tile_now = lax.dynamic_slice_in_dim(impacts, start, step)
        picked = jnp.take(grouped, term_now, axis=1)
        product = jnp.einsum("qnk,nkd->ndq", picked, tile_now, preferred_element_type=jnp.float32)
        select = ((owner_now[:, None] == owner_ids[None, :]) & keep_now[:, None]).astype(
            jnp.float32
        )
        added = jnp.einsum("ndq,nb->bdq", product, select, precision=lax.Precision.HIGHEST)
        return (total + added, None)

    start_total = jnp.zeros((owners, doc_block, queries), jnp.float32)
    total, unused = lax.scan(accumulate, start_total, jnp.arange(tiles // step, dtype=jnp.int32))
    partial_value = total.reshape(owners * doc_block, queries)
    mine = lax.psum_scatter(partial_value, "doc", scatter_dimension=0, tiled=True)
    scores = lax.psum(mine, "term")
    return scores


def solution(mesh):
    return jax.shard_map(
        per_device,
        mesh=mesh,
        in_specs=(
            P("enc", ("term", "doc")),
            P(("term", "doc")),
            P(("term", "doc")),
            P(("term", "doc")),
            P(("term", "doc"), None, None),
        ),
        out_specs=P("doc", "enc"),
        check_vma=False,
    )
```

profile of v0, /device:TPU:2, one launch (start us, length us, event | category | flops | bytes accessed | tf_op | source)
XLA Modules:
  0.0 312.8 jit_solution(1491762189442942286)
XLA Ops:
  6.5 0.7 all-gather.2.cloned.1.call-update
  8.0 78.3 %all-gather.2.cloned.1.call-done = bf16[256,3840]{0,1:T(8,128)(2,1)} async-done(((bf16[256,240]{0,1:T(8,128)(2,1)}), bf16[256,3840]{0,1:T(8,128)(2,1)}) %all-gather.2.cloned.1.call-update) | async-done | bytes 1966096 | tf_op jit(solution)/shard_map/all_gather | solution.py:16
  86.2 67.8 %while.11 = (s32[]{:T(128)}, f32[16,128,256]{2,0,1:T(8,128)}, s32[4]{0:T(128)S(1)}, s32[240]{0:T(256)}, pred[240]{0:T(512)(128)(4,1)S(1)}, /*index=5*/bf16[240,6...) while((s32[]{:T(128)}, f32[16,128,256]{2,0,1:T(8,128)}, ...), condition=%wide.region_1.2_spmd.clone, body=%wide.region_0.1_spmd.clone.sunk | while | flops 631180544 | bytes 43587780 | solution.py:40
  86.2 0.6 dynamic_slice.30
  87.6 0.8 dynamic_slice.31
  88.3 0.8 compare_and_fusion.2
  89.1 2.2 gather_fusion
  91.3 2.6 fusion.28
  93.9 7.9 %select_add_fusion.2 = f32[16,128,256]{2,0,1:T(8,128)S(1)} fusion(f32[16,128,256]{2,0,1:T(8,128)S(1)} %copy-done, f32[60,128,256]{2,1,0:T(8,128)S(1)} %fusion.28, pred[]{:T(512)S(6)} %compare.3, s32[60]{0:T(128)S(1)} %dynamic_slice.31, pred[60]{0:T(512)(128)(4,1)S(1)} %dynamic_slice.32), kind=kOutput, calls=%fused_computation.4.clone.1 | convolution fusion | flops 378537856 | bytes 12058925 | tf_op jit(solution)/shard_map/while/body/eval_jaxpr/ndq,nb->bdq/dot_general | solution.py:36
  101.9 1.3 copy-done.1
  104.5 0.8 dynamic_slice.31
  105.2 0.8 compare_and_fusion.2
  106.0 2.2 gather_fusion
  108.3 2.6 fusion.28
  110.9 7.9 %select_add_fusion.2 = f32[16,128,256]{2,0,1:T(8,128)S(1)} fusion(f32[16,128,256]{2,0,1:T(8,128)S(1)} %copy-done, f32[60,128,256]{2,1,0:T(8,128)S(1)} %fusion.28, pred[]{:T(512)S(6)} %compare.3, s32[60]{0:T(128)S(1)} %dynamic_slice.31, pred[60]{0:T(512)(128)(4,1)S(1)} %dynamic_slice.32), kind=kOutput, calls=%fused_computation.4.clone.1 | convolution fusion | flops 378537856 | bytes 12058925 | tf_op jit(solution)/shard_map/while/body/eval_jaxpr/ndq,nb->bdq/dot_general | solution.py:36
  118.8 1.3 copy-done.1
  121.4 0.8 dynamic_slice.31
  122.2 0.8 compare_and_fusion.2
  122.9 2.2 gather_fusion
  125.2 2.6 fusion.28
  127.8 7.9 %select_add_fusion.2 = f32[16,128,256]{2,0,1:T(8,128)S(1)} fusion(f32[16,128,256]{2,0,1:T(8,128)S(1)} %copy-done, f32[60,128,256]{2,1,0:T(8,128)S(1)} %fusion.28, pred[]{:T(512)S(6)} %compare.3, s32[60]{0:T(128)S(1)} %dynamic_slice.31, pred[60]{0:T(512)(128)(4,1)S(1)} %dynamic_slice.32), kind=kOutput, calls=%fused_computation.4.clone.1 | convolution fusion | flops 378537856 | bytes 12058925 | tf_op jit(solution)/shard_map/while/body/eval_jaxpr/ndq,nb->bdq/dot_general | solution.py:36
  135.7 1.3 copy-done.1
  138.4 0.8 dynamic_slice.31
  139.1 0.8 compare_and_fusion.2
  139.9 2.2 gather_fusion
  142.1 2.6 fusion.28
  144.8 7.9 %select_add_fusion.2 = f32[16,128,256]{2,0,1:T(8,128)S(1)} fusion(f32[16,128,256]{2,0,1:T(8,128)S(1)} %copy-done, f32[60,128,256]{2,1,0:T(8,128)S(1)} %fusion.28, pred[]{:T(512)S(6)} %compare.3, s32[60]{0:T(128)S(1)} %dynamic_slice.31, pred[60]{0:T(512)(128)(4,1)S(1)} %dynamic_slice.32), kind=kOutput, calls=%fused_computation.4.clone.1 | convolution fusion | flops 378537856 | bytes 12058925 | tf_op jit(solution)/shard_map/while/body/eval_jaxpr/ndq,nb->bdq/dot_general | solution.py:36
  152.7 1.3 copy-done.1
  154.0 4.1 %copy.8 = f32[16,128,256]{2,1,0:T(8,128)} copy(f32[16,128,256]{2,0,1:T(8,128)} %get-tuple-element.52) | data formatting | bytes 4194304 | tf_op jit(solution)/shard_map/while | solution.py:40
  158.2 71.0 %reduce-scatter.2.cloned.1.call-done = f32[128,256]{1,0:T(8,128)} async-done(((f32[2048,256]{1,0:T(8,128)}), f32[128,256]{1,0:T(8,128)}) %reduce-scatter.2.cloned.1.call-update) | async-done | bytes 131088 | tf_op jit(solution)/shard_map/reduce_scatter | solution.py:42
  229.3 75.4 %all-reduce.2.cloned.1.call-done = f32[128,256]{1,0:T(8,128)} async-done(((f32[128,256]{1,0:T(8,128)}), f32[128,256]{1,0:T(8,128)}) %all-reduce.2.cloned.1.call-update) | async-done | bytes 131088 | tf_op jit(solution)/shard_map/psum | solution.py:43
  304.7 1.6 copy.24
  (31 shorter events, 2.3 us)
Async XLA Ops:
  6.5 79.7 %all-gather.2.cloned.1.call-start = ((), (), s32[]{:S(2)}) async-start(), calls=%async_computation.1 | async-start | bytes 2088960 | tf_op jit(solution)/shard_map/all_gather | solution.py:16
  7.3 222.0 %reduce-scatter.2.cloned.1.call-start = ((), (), s32[]{:S(2)}) async-start(), calls=%async_computation.2 | async-start | bytes 2228224 | tf_op jit(solution)/shard_map/reduce_scatter | solution.py:42
  91.3 2.6 copy-start
  101.8 1.3 copy-start.1
  108.2 2.6 copy-start
  118.8 1.3 copy-start.1
  125.2 2.6 copy-start
  135.7 1.3 copy-start.1
  142.1 2.6 copy-start
  152.7 1.3 copy-start.1
  158.2 146.6 %all-reduce.2.cloned.1.call-start = ((), (), s32[]{:S(2)}) async-start(), calls=%async_computation.3 | async-start | bytes 262144 | tf_op jit(solution)/shard_map/psum | solution.py:43
Sparse Core Ops, SparseCore 0:
  9.4 76.7 all-gather.1
  158.3 70.9 reduce-scatter.1
  231.6 73.0 all-reduce.1
where the time goes:
time: 313 us
  waiting for transfers between devices  225 us (72%)
  matrix products  42 us (13%)
  local copies, waits for them, and re-layouts  25.7 us (8%)
  between operations  13.8 us (4%)
    all_gather x1, waiting for transfers between devices, per_device(): range_rows = lax.all_gather(query_weights, 'doc', axis=1, tiled=True)  78.3 us
    psum x1, waiting for transfers between devices, per_device(): scores = lax.psum(mine, 'term')  75.4 us
    reduce_scatter x1, waiting for transfers between devices, per_device(): lax.psum_scatter(partial_value, 'doc', scatter_dimension=0, tiled=True)  71 us
    dot_general x4, matrix products, accumulate(): jnp.einsum('ndq,nb->bdq', product, select, precision=lax.Precision.HIGHEST)  31.6 us
    dot_general x4, matrix products, accumulate(): jnp.einsum('qnk,nkd->ndq', picked, tile_now, preferred_element_type=jnp.f...  10.5 us
    gather x4, local copies, waits for them, and re-layouts, accumulate(): picked = jnp.take(grouped, term_now, axis=1)  8.92 us
  transfers between devices with their start and end apart: 3, of which 3 were waited for; matrix products, arithmetic and copies ran while one was open for 0% of the time, Pallas kernels for 0%

commit v1 on v0

--- a/solution.py
+++ b/solution.py
@@ -40,7 +40,10 @@
     total, unused = lax.scan(accumulate, start_total, jnp.arange(tiles // step, dtype=jnp.int32))
     partial_value = total.reshape(owners * doc_block, queries)
     mine = lax.psum_scatter(partial_value, "doc", scatter_dimension=0, tiled=True)
-    scores = lax.psum(mine, "term")
+    count, scores = (lax.axis_size("term"), mine)
+    for far in [1 << k for k in range(count.bit_length() - 1)]:
+        swap = [(i, i ^ far) for i in range(count)]
+        scores = scores + lax.ppermute(scores, "term", swap)
     return scores
 
 

time: 313 us -> 257 us (0.82)
  waiting for transfers between devices: 225 us -> 159 us
  starting transfers between devices: 0.08 us -> 9.99 us
    psum x1 -> x0, waiting for transfers between devices: 75.4 us -> none  [per_device(): scores = lax.psum(mine, 'term')]
    ppermute x0 -> x3, starting transfers between devices: none -> 9.95 us  [per_device(): scores = scores + lax.ppermute(scores, 'term', swap)]
    ppermute x0 -> x3, waiting for transfers between devices: none -> 9.28 us  [per_device(): scores = scores + lax.ppermute(scores, 'term', swap)]
  transfers between devices with their start and end apart: 3 -> 5, of which waited for: 3 -> 5; matrix products, arithmetic and copies ran while one was open for 0% -> 0% of each run, Pallas kernels for 0% -> 0%
where the time goes in v1:
time: 257 us
  waiting for transfers between devices  159 us (62%)
  matrix products  42 us (16%)
  local copies, waits for them, and re-layouts  24 us (9%)
  between operations  14.1 us (5%)
  starting transfers between devices  9.99 us (4%)
  other arithmetic  4.67 us (2%)
    all_gather x1, waiting for transfers between devices, per_device(): range_rows = lax.all_gather(query_weights, 'doc', axis=1, tiled=True)  78.3 us
    reduce_scatter x1, waiting for transfers between devices, per_device(): lax.psum_scatter(partial_value, 'doc', scatter_dimension=0, tiled=True)  71.2 us
    dot_general x4, matrix products, accumulate(): jnp.einsum('ndq,nb->bdq', product, select, precision=lax.Precision.HIGHEST)  31.6 us
    dot_general x4, matrix products, accumulate(): jnp.einsum('qnk,nkd->ndq', picked, tile_now, preferred_element_type=jnp.f...  10.5 us
    ppermute x3, starting transfers between devices, per_device(): scores = scores + lax.ppermute(scores, 'term', swap)  9.95 us
    ppermute x3, waiting for transfers between devices, per_device(): scores = scores + lax.ppermute(scores, 'term', swap)  9.28 us
    gather x4, local copies, waits for them, and re-layouts, accumulate(): picked = jnp.take(grouped, term_now, axis=1)  8.92 us
    while x16, local copies, waits for them, and re-layouts  5.32 us
  transfers between devices with their start and end apart: 5, of which 5 were waited for; matrix products, arithmetic and copies ran while one was open for 0% of the time, Pallas kernels for 0%

profile of v1, /device:TPU:2, one launch (start us, length us, event | category | flops | bytes accessed | tf_op | source)
XLA Modules:
  0.0 256.7 jit_solution(13428880006579317802)
XLA Ops:
  8.0 78.3 %all-gather.2.cloned.1.call-done = bf16[256,3840]{0,1:T(8,128)(2,1)} async-done(((bf16[256,240]{0,1:T(8,128)(2,1)}), bf16[256,3840]{0,1:T(8,128)(2,1)}) %all-gather.2.cloned.1.call-update) | async-done | bytes 1966096 | tf_op jit(solution)/shard_map/all_gather | solution.py:16
  86.2 67.4 %while.11 = (s32[]{:T(128)}, f32[16,128,256]{2,0,1:T(8,128)}, s32[4]{0:T(128)S(1)}, s32[240]{0:T(256)}, pred[240]{0:T(512)(128)(4,1)S(1)}, /*index=5*/bf16[240,6...) while((s32[]{:T(128)}, f32[16,128,256]{2,0,1:T(8,128)}, ...), condition=%wide.region_1.2_spmd.clone, body=%wide.region_0.1_spmd.clone.sunk | while | flops 631180544 | bytes 43587780 | solution.py:40
  87.5 0.8 dynamic_slice.31
  88.2 0.8 compare_and_fusion.2
  89.0 2.2 gather_fusion
  91.2 2.6 %fusion.28 = f32[60,128,256]{2,1,0:T(8,128)S(1)} fusion(bf16[60,256,64]{1,2,0:T(8,128)(2,1)S(1)} %gather_fusion, pred[60]{0:T(512)(128)(4,1)S(1)} %get-tuple-element.152, bf16[240,64,128]{2,1,0:T(8,128)(2,1)} %get-tuple-element.182, s32[]{:T(128)S(6)} %select_n.28), kind=kOutput, calls=%fused_computation.5.clone.1 | convolution fusion | flops 252641280 | bytes 10813504 | tf_op jit(solution)/shard_map/while/body/eval_jaxpr/qnk,nkd->ndq/dot_general | solution.py:32
  93.9 7.9 %select_add_fusion.2 = f32[16,128,256]{2,0,1:T(8,128)S(1)} fusion(f32[16,128,256]{2,0,1:T(8,128)S(1)} %copy-done, f32[60,128,256]{2,1,0:T(8,128)S(1)} %fusion.28, pred[]{:T(512)S(6)} %compare.3, s32[60]{0:T(128)S(1)} %dynamic_slice.31, pred[60]{0:T(512)(128)(4,1)S(1)} %dynamic_slice.32), kind=kOutput, calls=%fused_computation.4.clone.1 | convolution fusion | flops 378537856 | bytes 12058925 | tf_op jit(solution)/shard_map/while/body/eval_jaxpr/ndq,nb->bdq/dot_general | solution.py:36
  101.8 1.3 copy-done.1
  105.1 0.8 compare_and_fusion.2
  105.9 2.2 gather_fusion
  108.1 2.6 %fusion.28 = f32[60,128,256]{2,1,0:T(8,128)S(1)} fusion(bf16[60,256,64]{1,2,0:T(8,128)(2,1)S(1)} %gather_fusion, pred[60]{0:T(512)(128)(4,1)S(1)} %get-tuple-element.152, bf16[240,64,128]{2,1,0:T(8,128)(2,1)} %get-tuple-element.182, s32[]{:T(128)S(6)} %select_n.28), kind=kOutput, calls=%fused_computation.5.clone.1 | convolution fusion | flops 252641280 | bytes 10813504 | tf_op jit(solution)/shard_map/while/body/eval_jaxpr/qnk,nkd->ndq/dot_general | solution.py:32
  110.7 7.9 %select_add_fusion.2 = f32[16,128,256]{2,0,1:T(8,128)S(1)} fusion(f32[16,128,256]{2,0,1:T(8,128)S(1)} %copy-done, f32[60,128,256]{2,1,0:T(8,128)S(1)} %fusion.28, pred[]{:T(512)S(6)} %compare.3, s32[60]{0:T(128)S(1)} %dynamic_slice.31, pred[60]{0:T(512)(128)(4,1)S(1)} %dynamic_slice.32), kind=kOutput, calls=%fused_computation.4.clone.1 | convolution fusion | flops 378537856 | bytes 12058925 | tf_op jit(solution)/shard_map/while/body/eval_jaxpr/ndq,nb->bdq/dot_general | solution.py:36
  118.6 1.3 copy-done.1
  122.0 0.8 compare_and_fusion.2
  122.7 2.2 gather_fusion
  125.0 2.6 %fusion.28 = f32[60,128,256]{2,1,0:T(8,128)S(1)} fusion(bf16[60,256,64]{1,2,0:T(8,128)(2,1)S(1)} %gather_fusion, pred[60]{0:T(512)(128)(4,1)S(1)} %get-tuple-element.152, bf16[240,64,128]{2,1,0:T(8,128)(2,1)} %get-tuple-element.182, s32[]{:T(128)S(6)} %select_n.28), kind=kOutput, calls=%fused_computation.5.clone.1 | convolution fusion | flops 252641280 | bytes 10813504 | tf_op jit(solution)/shard_map/while/body/eval_jaxpr/qnk,nkd->ndq/dot_general | solution.py:32
  127.6 7.9 %select_add_fusion.2 = f32[16,128,256]{2,0,1:T(8,128)S(1)} fusion(f32[16,128,256]{2,0,1:T(8,128)S(1)} %copy-done, f32[60,128,256]{2,1,0:T(8,128)S(1)} %fusion.28, pred[]{:T(512)S(6)} %compare.3, s32[60]{0:T(128)S(1)} %dynamic_slice.31, pred[60]{0:T(512)(128)(4,1)S(1)} %dynamic_slice.32), kind=kOutput, calls=%fused_computation.4.clone.1 | convolution fusion | flops 378537856 | bytes 12058925 | tf_op jit(solution)/shard_map/while/body/eval_jaxpr/ndq,nb->bdq/dot_general | solution.py:36
  135.5 1.3 copy-done.1
  138.8 0.8 compare_and_fusion.2
  139.6 2.2 gather_fusion
  141.8 2.6 %fusion.28 = f32[60,128,256]{2,1,0:T(8,128)S(1)} fusion(bf16[60,256,64]{1,2,0:T(8,128)(2,1)S(1)} %gather_fusion, pred[60]{0:T(512)(128)(4,1)S(1)} %get-tuple-element.152, bf16[240,64,128]{2,1,0:T(8,128)(2,1)} %get-tuple-element.182, s32[]{:T(128)S(6)} %select_n.28), kind=kOutput, calls=%fused_computation.5.clone.1 | convolution fusion | flops 252641280 | bytes 10813504 | tf_op jit(solution)/shard_map/while/body/eval_jaxpr/qnk,nkd->ndq/dot_general | solution.py:32
  144.5 7.9 %select_add_fusion.2 = f32[16,128,256]{2,0,1:T(8,128)S(1)} fusion(f32[16,128,256]{2,0,1:T(8,128)S(1)} %copy-done, f32[60,128,256]{2,1,0:T(8,128)S(1)} %fusion.28, pred[]{:T(512)S(6)} %compare.3, s32[60]{0:T(128)S(1)} %dynamic_slice.31, pred[60]{0:T(512)(128)(4,1)S(1)} %dynamic_slice.32), kind=kOutput, calls=%fused_computation.4.clone.1 | convolution fusion | flops 378537856 | bytes 12058925 | tf_op jit(solution)/shard_map/while/body/eval_jaxpr/ndq,nb->bdq/dot_general | solution.py:36
  152.4 1.3 copy-done.1
  153.7 4.1 %copy.8 = f32[16,128,256]{2,1,0:T(8,128)} copy(f32[16,128,256]{2,0,1:T(8,128)} %get-tuple-element.52) | data formatting | bytes 4194304 | tf_op jit(solution)/shard_map/while | solution.py:40
  157.8 71.2 %reduce-scatter.2.cloned.1.call-done = f32[128,256]{1,0:T(8,128)} async-done(((f32[2048,256]{1,0:T(8,128)}), f32[128,256]{1,0:T(8,128)}) %reduce-scatter.2.cloned.1.call-update) | async-done | bytes 131088 | tf_op jit(solution)/shard_map/reduce_scatter | solution.py:42
  229.0 1.9 collective-permute-start
  230.9 1.5 collective-permute-done
  232.5 0.9 add.31
  233.4 3.3 %collective-permute-start.1 = (f32[128,256]{1,0:T(8,128)S(1)}, f32[128,256]{1,0:T(8,128)S(1)}, u32[]{:S(2)}, u32[]{:S(2)}) collective-permute-start(f32[128,256]{1,0:T(8,128)S(1)} %add.31), channel_id=1, source_target_pairs={{0,128},{64,192},{128,0},{192,64},{256,384},{320,448},{384,256},{4... | collective-permute-start | bytes 393224 | tf_op jit(solution)/shard_map/ppermute | solution.py:46
  236.7 4.2 %collective-permute-done.1 = f32[128,256]{1,0:T(8,128)S(1)} collective-permute-done((f32[128,256]{1,0:T(8,128)S(1)}, f32[128,256]{1,0:T(8,128)S(1)}, u32[]{:S(2)}, u32[]{:S(2)}) %collective-permute-start.1) | collective-permute-done | bytes 131104 | tf_op jit(solution)/shard_map/ppermute | solution.py:46
  240.9 4.8 %collective-permute-start.2 = (f32[128,256]{1,0:T(8,128)S(1)}, f32[128,256]{1,0:T(8,128)S(1)}, u32[]{:S(2)}, u32[]{:S(2)}) collective-permute-start(f32[128,256]{1,0:T(8,128)S(1)} %add.32), channel_id=1, source_target_pairs={{0,256},{64,320},{128,384},{192,448},{256,0},{320,64},{384,128},{4... | collective-permute-start | bytes 393224 | tf_op jit(solution)/shard_map/ppermute | solution.py:46
  245.7 3.6 %collective-permute-done.2 = f32[128,256]{1,0:T(8,128)S(1)} collective-permute-done((f32[128,256]{1,0:T(8,128)S(1)}, f32[128,256]{1,0:T(8,128)S(1)}, u32[]{:S(2)}, u32[]{:S(2)}) %collective-permute-start.2) | collective-permute-done | bytes 131104 | tf_op jit(solution)/shard_map/ppermute | solution.py:46
  (36 shorter events, 6.4 us)
Async XLA Ops:
  6.5 79.7 %all-gather.2.cloned.1.call-start = ((), (), s32[]{:S(2)}) async-start(), calls=%async_computation.1 | async-start | bytes 2088960 | tf_op jit(solution)/shard_map/all_gather | solution.py:16
  7.3 221.8 %reduce-scatter.2.cloned.1.call-start = ((), (), s32[]{:S(2)}) async-start(), calls=%async_computation.2 | async-start | bytes 2228224 | tf_op jit(solution)/shard_map/reduce_scatter | solution.py:42
  91.2 2.6 %copy-start = (f32[16,128,256]{2,0,1:T(8,128)S(1)}, f32[16,128,256]{2,0,1:T(8,128)}, u32[]{:S(2)}) copy-start(f32[16,128,256]{2,0,1:T(8,128)} %get-tuple-element.166) | copy-start | bytes 6291460 | tf_op jit(solution)/shard_map/while
  101.8 1.3 copy-start.1
  108.1 2.6 %copy-start = (f32[16,128,256]{2,0,1:T(8,128)S(1)}, f32[16,128,256]{2,0,1:T(8,128)}, u32[]{:S(2)}) copy-start(f32[16,128,256]{2,0,1:T(8,128)} %get-tuple-element.166) | copy-start | bytes 6291460 | tf_op jit(solution)/shard_map/while
  118.6 1.3 copy-start.1
  125.0 2.6 %copy-start = (f32[16,128,256]{2,0,1:T(8,128)S(1)}, f32[16,128,256]{2,0,1:T(8,128)}, u32[]{:S(2)}) copy-start(f32[16,128,256]{2,0,1:T(8,128)} %get-tuple-element.166) | copy-start | bytes 6291460 | tf_op jit(solution)/shard_map/while
  135.5 1.3 copy-start.1
  141.8 2.6 %copy-start = (f32[16,128,256]{2,0,1:T(8,128)S(1)}, f32[16,128,256]{2,0,1:T(8,128)}, u32[]{:S(2)}) copy-start(f32[16,128,256]{2,0,1:T(8,128)} %get-tuple-element.166) | copy-start | bytes 6291460 | tf_op jit(solution)/shard_map/while
  152.4 1.3 copy-start.1
  229.0 3.4 %collective-permute-start = (f32[128,256]{1,0:T(8,128)}, f32[128,256]{1,0:T(8,128)S(1)}, u32[]{:S(2)}, u32[]{:S(2)}) collective-permute-start(f32[128,256]{1,0:T(8,128)} %reduce-scatter.2.cloned.1.call-done), channel_id=1, source_target_pairs={{0,64},{64,0},{128,192},{192,128},{256,320},{320,256},{384,448},{4... | collective-permute-start | bytes 393224 | tf_op jit(solution)/shard_map/ppermute | solution.py:46
  233.4 7.4 %collective-permute-start.1 = (f32[128,256]{1,0:T(8,128)S(1)}, f32[128,256]{1,0:T(8,128)S(1)}, u32[]{:S(2)}, u32[]{:S(2)}) collective-permute-start(f32[128,256]{1,0:T(8,128)S(1)} %add.31), channel_id=1, source_target_pairs={{0,128},{64,192},{128,0},{192,64},{256,384},{320,448},{384,256},{4... | collective-permute-start | bytes 393224 | tf_op jit(solution)/shard_map/ppermute | solution.py:46
  240.9 8.4 %collective-permute-start.2 = (f32[128,256]{1,0:T(8,128)S(1)}, f32[128,256]{1,0:T(8,128)S(1)}, u32[]{:S(2)}, u32[]{:S(2)}) collective-permute-start(f32[128,256]{1,0:T(8,128)S(1)} %add.32), channel_id=1, source_target_pairs={{0,256},{64,320},{128,384},{192,448},{256,0},{320,64},{384,128},{4... | collective-permute-start | bytes 393224 | tf_op jit(solution)/shard_map/ppermute | solution.py:46
Sparse Core Ops, SparseCore 0:
  9.4 76.7 all-gather.1
  158.0 71.0 reduce-scatter.1
